TPU v7x, 32 devices: a whole 2x2x4 slice. The times are simulated.
32 devices in a mesh: wide: 8 (over z, x), narrow: 4 (over y, core).
Axes of the slice: x: 2, y: 2, z: 4, core: 2. Of those that a mesh axis runs over, the one named last changes fastest.
Arguments:
- pressure: float32 [1024, 128], P(('wide', 'narrow')), may hold values from -6 to 6
- right_side: float32 [1024, 128], P(('wide', 'narrow')), may hold values from -6 to 6
- concentration: float32 [1024, 128], P(('wide', 'narrow')), may hold values from 0 to 1
- pore_volume: float32 [1024, 128], P(('wide', 'narrow')), may hold values from 0.5 to 2
- well_rate: float32 [1024, 128], P(('wide', 'narrow')), may hold values from 0.02 to 0.5
- inject_conc: float32 [1024, 128], P(('wide', 'narrow')), may hold values from 0 to 1
- transmissibility: float32 [6, 131072], P(None, ('wide', 'narrow')), may hold values from 0.1 to 1
- face_neighbor: int32 [6, 1024], P(None, ('wide', 'narrow')), may hold values from 0 to 56, as said below
- sub_matrix: bfloat16 [2048, 4, 128, 128], P(('wide', 'narrow')), as said below
- sub_columns: int32 [2048, 4], P(('wide', 'narrow')), may hold values from 0 to 63, as said below
- send_blocks: int32 [32, 4, 8], P(('wide', 'narrow')), may hold values from 0 to 31, as said below
- send_counts: int32 [32, 4], P(('wide', 'narrow')), may hold values from 1 to 8, as said below
- basis_weights: bfloat16 [8192, 4096], P(('wide', 'narrow')), may hold values from -0.09375 to 0.09375
- coarse_index: int32 [8192], P(('wide', 'narrow')), may hold values from 0 to 4095, as said below
- coarse_inverse: float32 [4096, 512], P(('wide', 'narrow')), may hold values from -0.25 to 0.25
Outputs:
- pressure_new: float32 [1024, 128], P(('wide', 'narrow'))
- concentration_new: float32 [1024, 128], P(('wide', 'narrow'))
Inputs may be any that keep to these rules, and one draw needn't show every extreme that they name: `send_blocks`: local block indices below 32. `send_counts`: between 1 and 8; the first subdomain sends 8 blocks to every neighbour and the last sends one. `sub_columns`: slot 0 of each row block names the row block itself. `face_neighbor`: each owned block's faces name owned blocks or the first received block from some neighbour. `coarse_index`: a subdomain's functions may be owned by any index of wide, and may repeat. `sub_matrix`: the diagonal of each row block's first stored block lies between 0.9 and 2.1.
All inputs are finite; a program needn't handle non-finite values.
Results may differ from a plain program's by a relative error of at most 0.00225.
The roundings to bfloat16 on the way count: a program that leaves them out, or rounds other values in their place, can miss the bound.
Values may be sent and summed in bfloat16 or wider, within the bound.
A program may use at most 64 MiB of HBM per device.

v0:
```python
import jax
import jax.numpy as jnp
from jax import lax
from jax.sharding import PartitionSpec as P

SWEEPS = 4
shift_offsets = (2, 1, -1, -2)
courant = 0.9


def from_behind(value, axis, steps):
    count = lax.axis_size(axis)
    leading, last = (max(0, -steps), min(count, count - steps))
    return lax.ppermute(value, axis, [(source, source + steps) for source in range(leading, last)])


def block_product(matrix, columns, vector_b):
    picked = vector_b[columns]
    return jnp.einsum("rkij,rkj->ri", matrix, picked, preferred_element_type=jnp.float32)


def outgoing_one(owned_rows, send_blocks, send_counts):
    slot_count = send_blocks.shape[-1]
    active = jnp.arange(slot_count)[None, :] < send_counts[0][:, None]
    picked = owned_rows[send_blocks[0]]
    return jnp.where(active[:, :, None], picked, jnp.zeros_like(picked))


def with_rims(owned_list, send_blocks, send_counts, mover):
    packed = [outgoing_one(owned_rows, send_blocks, send_counts) for owned_rows in owned_list]
    arrived = [[owned_rows] for owned_rows in owned_list]
    for position, offset in enumerate(shift_offsets):
        moved_rows = mover([sent_rows[position] for sent_rows in packed], offset)
        for target, portion in zip(arrived, moved_rows):
            target.append(portion)
    return [jnp.concatenate(target, axis=0) for target in arrived]


def local(
    pressure,
    right_side,
    concentration,
    pore_volume,
    well_rate,
    inject_conc,
    transmissibility,
    face_neighbor,
    sub_matrix,
    sub_columns,
    send_blocks,
    send_counts,
    basis_weights,
    coarse_index,
    coarse_inverse,
):
    owned_count = pressure.shape[0]
    pressure_b = pressure.astype(jnp.bfloat16)
    ext_pressure = with_rims(
        [pressure_b],
        send_blocks,
        send_counts,
        lambda members, offset: (from_behind(members[0], "wide", offset),),
    )[0]
    residual = right_side - block_product(
        sub_matrix[:owned_count], sub_columns[:owned_count], ext_pressure
    )
    residual_b = residual.astype(jnp.bfloat16)
    local_coarse = jnp.dot(
        basis_weights, residual_b.reshape(-1), preferred_element_type=jnp.float32
    )
    coarse_width = coarse_inverse.shape[1]
    wide_count = lax.axis_size("wide")
    coarse_total = coarse_width * wide_count
    ext_residual = with_rims(
        [residual_b],
        send_blocks,
        send_counts,
        lambda members, offset: (from_behind(members[0], "wide", offset),),
    )[0]
    diagonal = jnp.diagonal(sub_matrix[:, 0], axis1=1, axis2=2).astype(jnp.float32)
    target_rows = ext_residual.astype(jnp.float32)
    update = jnp.zeros(target_rows.shape, jnp.float32)
    for turn_index in range(SWEEPS):
        update = (
            update
            + (target_rows - block_product(sub_matrix, sub_columns, update.astype(jnp.bfloat16)))
            / diagonal
        )
    partial_value = jnp.zeros((coarse_total,), jnp.float32).at[coarse_index].add(local_coarse)
    summed = lax.psum(partial_value, ("wide", "narrow"))
    owner_block = lax.dynamic_slice_in_dim(
        summed, lax.axis_index("wide") * coarse_width, coarse_width
    )
    block_inverse = lax.all_gather(coarse_inverse, "narrow", axis=0, tiled=True)
    owner_values = jnp.dot(block_inverse, owner_block, precision=lax.Precision.HIGHEST)
    coarse_values = lax.all_gather(owner_values, "wide", axis=0, tiled=True)
    picked_coarse = coarse_values.astype(jnp.bfloat16)[coarse_index]
    correction = jnp.dot(picked_coarse, basis_weights, preferred_element_type=jnp.float32)
    pressure_next = pressure + update[:owned_count] + correction.reshape(owned_count, -1)
    ext_next, ext_conc = with_rims(
        [pressure_next, concentration],
        send_blocks,
        send_counts,
        lambda members, offset: from_behind((members[0], members[1]), "wide", offset),
    )
    face_count = face_neighbor.shape[0]
    near_pressure = ext_next[face_neighbor].reshape(face_count, -1)
    near_conc = ext_conc[face_neighbor].reshape(face_count, -1)
    own_pressure = pressure_next.reshape(1, -1)
    conc_flat = concentration.reshape(-1)
    face_flux = transmissibility * (own_pressure - near_pressure)
    outward = jnp.maximum(face_flux, 0.0)
    inward = jnp.minimum(face_flux, 0.0)
    advection = jnp.sum(outward * conc_flat[None, :] + inward * near_conc, axis=0)
    outflow = jnp.sum(outward, axis=0)
    volume_flat = pore_volume.reshape(-1)
    rate_flat = well_rate.reshape(-1)
    cell_rate = (outflow + rate_flat) / volume_flat
    rate_top = lax.pmax(jnp.max(cell_rate), ("wide", "narrow"))
    time_step = courant / rate_top
    conc_next = conc_flat + time_step / volume_flat * (
        rate_flat * (inject_conc.reshape(-1) - conc_flat) - advection
    )
    return (pressure_next, conc_next.reshape(owned_count, -1))


def solution(mesh):
    return jax.shard_map(
        local,
        mesh=mesh,
        in_specs=(
            P(("wide", "narrow"), None),
            P(("wide", "narrow"), None),
            P(("wide", "narrow"), None),
            P(("wide", "narrow"), None),
            P(("wide", "narrow"), None),
            P(("wide", "narrow"), None),
            P(None, ("wide", "narrow")),
            P(None, ("wide", "narrow")),
            P(("wide", "narrow"), None, None, None),
            P(("wide", "narrow"), None),
            P(("wide", "narrow"), None, None),
            P(("wide", "narrow"), None),
            P(("wide", "narrow"), None),
            P(("wide", "narrow")),
            P(("wide", "narrow"), None),
        ),
        out_specs=(P(("wide", "narrow"), None), P(("wide", "narrow"), None)),
        check_vma=False,
    )
```

profile of v0, /device:TPU:0, one launch (start us, length us, event | category | flops | bytes accessed | tf_op | source)
XLA Modules:
  0.0 232.3 jit_solution(17184199817668447989)
XLA Ops:
  7.2 0.9 constant_dynamic-update-slice_fusion.4
  8.1 0.7 compare_select_fusion.3
  8.9 0.7 iota_compare_fusion
  10.3 4.9 %collective-permute-start = (bf16[8,128]{1,0:T(8,128)(2,1)S(1)}, bf16[8,128]{1,0:T(8,128)(2,1)S(1)}, u32[]{:S(2)}, u32[]{:S(2)}) collective-permute-start(bf16[8,128]{1,0:T(8,128)(2,1)S(1)} %get-tuple-element.29), channel_id=1, source_target_pairs={{0,8},{4,12},{8,16},{12,20},{16,24},{20,28},{1,9},{5,13},{9,17},{1... | collective-permute-start | bytes 6152 | tf_op jit(solution)/shard_map/ppermute | solution.py:14
  15.2 3.4 %collective-permute-start.1 = (bf16[8,128]{1,0:T(8,128)(2,1)S(1)}, bf16[8,128]{1,0:T(8,128)(2,1)S(1)}, u32[]{:S(2)}, u32[]{:S(2)}) collective-permute-start(bf16[8,128]{1,0:T(8,128)(2,1)S(1)} %get-tuple-element.28), channel_id=1, source_target_pairs={{0,4},{4,8},{8,12},{12,16},{16,20},{20,24},{24,28},{1,5},{5,9},{9,... | collective-permute-start | bytes 6152 | tf_op jit(solution)/shard_map/ppermute | solution.py:14
  18.6 1.3 collective-permute-start.2
  19.9 1.3 collective-permute-start.3
  21.2 0.7 compare_select_fusion.2
  21.9 0.7 compare_select_fusion.1
  22.6 0.7 compare_select_fusion.4
  23.5 3.2 %slice.70 = bf16[64,1,128,128]{3,2,1,0:T(8,128)(2,1)} slice(bf16[64,4,128,128]{3,2,1,0:T(8,128)(2,1)} %param.23), slice={[0:64], [0:1], [0:128], [0:128]} | slice | bytes 4194304 | tf_op jit(solution)/shard_map/slice | solution.py:80
  26.7 5.3 %copy.38 = bf16[64,1,128,128]{0,3,2,1:T(8,128)(2,1)} copy(bf16[64,1,128,128]{3,2,1,0:T(8,128)(2,1)} %slice.70) | data formatting | bytes 4194304
  32.1 1.9 gather_fusion.4
  34.4 0.9 gather_fusion.3
  35.2 5.7 %fusion.8 = f32[64,1,128,1]{2,1,3,0:T(1,128)S(1)} fusion(bf16[64,4,128,128]{3,2,1,0:T(8,128)(2,1)} %param.23, bf16[64,4,128,1]{2,1,0,3:T(4,128)(2,1)S(1)} %bitcast.134), kind=kOutput, calls=%fused_computation.23 | convolution fusion | flops 8388608 | bytes 8486912 | tf_op jit(solution)/shard_map/rkij,rkj->ri/dot_general | solution.py:19
  41.7 0.7 gather_fusion.1
  42.4 3.4 %fusion = f32[32,1,128,1]{2,1,3,0:T(1,128)S(1)} fusion(bf16[64,4,128,128]{3,2,1,0:T(8,128)(2,1)} %param.23, bf16[32,4,128,1]{2,1,0,3:T(4,128)(2,1)S(1)} %bitcast.143), kind=kOutput, calls=%fused_computation.14 | convolution fusion | flops 4194304 | bytes 4243456 | tf_op jit(solution)/shard_map/rkij,rkj->ri/dot_general | solution.py:19
  46.5 6.3 %collective-permute-start.4 = (bf16[8,128]{1,0:T(8,128)(2,1)S(1)}, bf16[8,128]{1,0:T(8,128)(2,1)S(1)}, u32[]{:S(2)}, u32[]{:S(2)}) collective-permute-start(bf16[8,128]{1,0:T(8,128)(2,1)S(1)} %get-tuple-element.25), channel_id=1, source_target_pairs={{0,8},{4,12},{8,16},{12,20},{16,24},{20,28},{1,9},{5,13},{9,17},{1... | collective-permute-start | bytes 6152 | tf_op jit(solution)/shard_map/ppermute | solution.py:14
  52.8 0.6 fusion.23
  53.5 2.0 scatter_custom_fusion
  55.4 40.0 %psum.7 = f32[4096]{0:T(1024)S(1)} all-reduce(f32[4096]{0:T(1024)S(1)} %scatter_custom_fusion), channel_id=1, replica_groups=mesh['wide'=8,'narrow'=4] {'wide','narrow'}, use_global_device_ids=true, to_apply=%region_1.2 | all-reduce | flops 4096 | bytes 32768 | tf_op jit(solution)/shard_map/psum | solution.py:90
  95.4 4.2 %collective-permute-start.5 = (bf16[8,128]{1,0:T(8,128)(2,1)S(1)}, bf16[8,128]{1,0:T(8,128)(2,1)S(1)}, u32[]{:S(2)}, u32[]{:S(2)}) collective-permute-start(bf16[8,128]{1,0:T(8,128)(2,1)S(1)} %get-tuple-element.24), channel_id=1, source_target_pairs={{0,4},{4,8},{8,12},{12,16},{16,20},{20,24},{24,28},{1,5},{5,9},{9,... | collective-permute-start | bytes 6152 | tf_op jit(solution)/shard_map/ppermute | solution.py:14
  99.6 1.3 collective-permute-start.6
  100.9 1.5 collective-permute-start.7
  102.5 2.6 %collective-permute-done.6 = bf16[8,128]{1,0:T(8,128)(2,1)S(1)} collective-permute-done((bf16[8,128]{1,0:T(8,128)(2,1)S(1)}, bf16[8,128]{1,0:T(8,128)(2,1)S(1)}, u32[]{:S(2)}, u32[]{:S(2)}) %collective-permute-start.6) | collective-permute-done | bytes 2080 | tf_op jit(solution)/shard_map/ppermute | solution.py:14
  105.1 1.4 collective-permute-done.7
  106.5 0.9 gather_fusion.5
  107.4 5.6 %fusion.6 = f32[64,1,128,1]{2,1,3,0:T(1,128)S(1)} fusion(bf16[64,4,128,128]{3,2,1,0:T(8,128)(2,1)} %param.23, bf16[64,4,128,1]{2,1,0,3:T(4,128)(2,1)S(1)} %bitcast.135), kind=kOutput, calls=%fused_computation.21 | convolution fusion | flops 8388608 | bytes 8486912 | tf_op jit(solution)/shard_map/rkij,rkj->ri/dot_general | solution.py:19
  113.0 0.9 gather_fusion.6
  113.9 5.6 %fusion.4 = f32[64,1,128,1]{2,1,3,0:T(1,128)S(1)} fusion(bf16[64,4,128,128]{3,2,1,0:T(8,128)(2,1)} %param.23, bf16[64,4,128,1]{2,1,0,3:T(4,128)(2,1)S(1)} %bitcast.136), kind=kOutput, calls=%fused_computation.19 | convolution fusion | flops 8388608 | bytes 8486912 | tf_op jit(solution)/shard_map/rkij,rkj->ri/dot_general | solution.py:19
  119.6 0.9 gather_fusion.7
  120.5 5.6 %fusion.2 = f32[64,1,128,1]{2,1,3,0:T(1,128)S(1)} fusion(bf16[64,4,128,128]{3,2,1,0:T(8,128)(2,1)} %param.23, bf16[64,4,128,1]{2,1,0,3:T(4,128)(2,1)S(1)} %bitcast.133), kind=kOutput, calls=%fused_computation.17 | convolution fusion | flops 8388608 | bytes 8486912 | tf_op jit(solution)/shard_map/rkij,rkj->ri/dot_general | solution.py:19
  126.1 2.2 convolution_bitcast_fusion
  128.3 26.0 %all-gather = bf16[8,1,512]{2,1,0:T(2,128)(2,1)S(1)} all-gather(bf16[1,1,512]{2,1,0:T(2,128)(2,1)S(1)} %convolution_bitcast_fusion), channel_id=1, replica_groups=mesh['wide'=8,'narrow'=4] {'wide'}, dimensions={0}, use_global_device_ids=true | all-gather | bytes 9216 | tf_op jit(solution)/shard_map/all_gather | solution.py:96
  154.4 1.9 gather_fusion.8
  157.4 2.1 collective-permute-start.8
  159.5 1.8 collective-permute-start.9
  161.3 1.3 collective-permute-start.10
  162.6 1.3 collective-permute-start.11
  163.9 6.5 %collective-permute-start.12 = (f32[8,128]{1,0:T(8,128)S(1)}, f32[8,128]{1,0:T(8,128)S(1)}, u32[]{:S(2)}, u32[]{:S(2)}) collective-permute-start(f32[8,128]{1,0:T(8,128)S(1)} %get-tuple-element.17), channel_id=1, source_target_pairs={{0,8},{4,12},{8,16},{12,20},{16,24},{20,28},{1,9},{5,13},{9,17},{1... | collective-permute-start | bytes 12296 | tf_op jit(solution)/shard_map/ppermute | solution.py:14
  170.4 2.6 %collective-permute-start.13 = (f32[8,128]{1,0:T(8,128)S(1)}, f32[8,128]{1,0:T(8,128)S(1)}, u32[]{:S(2)}, u32[]{:S(2)}) collective-permute-start(f32[8,128]{1,0:T(8,128)S(1)} %get-tuple-element.16), channel_id=1, source_target_pairs={{0,4},{4,8},{8,12},{12,16},{16,20},{20,24},{24,28},{1,5},{5,9},{9,... | collective-permute-start | bytes 12296 | tf_op jit(solution)/shard_map/ppermute | solution.py:14
  173.1 1.3 collective-permute-start.14
  174.4 1.3 collective-permute-start.15
  175.8 3.5 %collective-permute-done.14 = f32[8,128]{1,0:T(8,128)S(1)} collective-permute-done((f32[8,128]{1,0:T(8,128)S(1)}, f32[8,128]{1,0:T(8,128)S(1)}, u32[]{:S(2)}, u32[]{:S(2)}) %collective-permute-start.14) | collective-permute-done | bytes 4128 | tf_op jit(solution)/shard_map/ppermute | solution.py:14
  179.3 0.7 gather_fusion.10
  180.0 2.7 %collective-permute-done.15 = f32[8,128]{1,0:T(8,128)S(1)} collective-permute-done((f32[8,128]{1,0:T(8,128)S(1)}, f32[8,128]{1,0:T(8,128)S(1)}, u32[]{:S(2)}, u32[]{:S(2)}) %collective-permute-start.15) | collective-permute-done | bytes 4128 | tf_op jit(solution)/shard_map/ppermute | solution.py:14
  182.7 0.7 gather_fusion.12
  184.2 39.9 %pmax.7 = f32[]{:T(128)} all-reduce(f32[]{:T(128)} %fusion.16), channel_id=1, replica_groups=mesh['wide'=8,'narrow'=4] {'wide','narrow'}, use_global_device_ids=true, to_apply=%region_4.5 | all-reduce | flops 1 | bytes 8 | tf_op jit(solution)/shard_map/pmax | solution.py:119
  (96 shorter events, 5.6 us)
Async XLA Ops:
  7.2 45.6 %copy-start = (bf16[256,4096]{1,0:T(8,128)(2,1)S(1)}, bf16[256,4096]{1,0:T(8,128)(2,1)}, u32[]{:S(2)}) copy-start(bf16[256,4096]{1,0:T(8,128)(2,1)} %param.27) | copy-start | bytes 6291460
  7.2 118.9 %all-gather.3.cloned.1.call-start = ((), (), s32[]{:S(2)}) async-start(), calls=%async_computation | async-start | bytes 1310720 | tf_op jit(solution)/shard_map/all_gather | solution.py:94
  10.3 31.3 %collective-permute-start = (bf16[8,128]{1,0:T(8,128)(2,1)S(1)}, bf16[8,128]{1,0:T(8,128)(2,1)S(1)}, u32[]{:S(2)}, u32[]{:S(2)}) collective-permute-start(bf16[8,128]{1,0:T(8,128)(2,1)S(1)} %get-tuple-element.29), channel_id=1, source_target_pairs={{0,8},{4,12},{8,16},{12,20},{16,24},{20,28},{1,9},{5,13},{9,17},{1... | collective-permute-start | bytes 6152 | tf_op jit(solution)/shard_map/ppermute | solution.py:14
  15.2 26.4 %collective-permute-start.1 = (bf16[8,128]{1,0:T(8,128)(2,1)S(1)}, bf16[8,128]{1,0:T(8,128)(2,1)S(1)}, u32[]{:S(2)}, u32[]{:S(2)}) collective-permute-start(bf16[8,128]{1,0:T(8,128)(2,1)S(1)} %get-tuple-element.28), channel_id=1, source_target_pairs={{0,4},{4,8},{8,12},{12,16},{16,20},{20,24},{24,28},{1,5},{5,9},{9,... | collective-permute-start | bytes 6152 | tf_op jit(solution)/shard_map/ppermute | solution.py:14
  18.6 23.0 %collective-permute-start.2 = (bf16[8,128]{1,0:T(8,128)(2,1)S(1)}, bf16[8,128]{1,0:T(8,128)(2,1)S(1)}, u32[]{:S(2)}, u32[]{:S(2)}) collective-permute-start(bf16[8,128]{1,0:T(8,128)(2,1)S(1)} %get-tuple-element.27), channel_id=1, source_target_pairs={{4,0},{8,4},{12,8},{16,12},{20,16},{24,20},{28,24},{5,1},{9,5},{13... | collective-permute-start | bytes 6152 | tf_op jit(solution)/shard_map/ppermute | solution.py:14
  19.9 21.8 %collective-permute-start.3 = (bf16[8,128]{1,0:T(8,128)(2,1)S(1)}, bf16[8,128]{1,0:T(8,128)(2,1)S(1)}, u32[]{:S(2)}, u32[]{:S(2)}) collective-permute-start(bf16[8,128]{1,0:T(8,128)(2,1)S(1)} %get-tuple-element.26), channel_id=1, source_target_pairs={{8,0},{12,4},{16,8},{20,12},{24,16},{28,20},{9,1},{13,5},{17,9},{2... | collective-permute-start | bytes 6152 | tf_op jit(solution)/shard_map/ppermute | solution.py:14
  26.7 14.2 %copy-start.9 = (s32[6,32]{1,0:T(8,128)S(1)}, s32[6,32]{1,0:T(8,128)}, u32[]{:S(2)}) copy-start(s32[6,32]{1,0:T(8,128)} %param.22) | copy-start | bytes 2308
  26.7 14.3 %copy-start.1 = (f32[32,128]{1,0:T(8,128)S(1)}, f32[32,128]{1,0:T(8,128)}, u32[]{:S(2)}) copy-start(f32[32,128]{1,0:T(8,128)} %param.17) | copy-start | bytes 49156
  32.1 13.7 %copy-start.7 = (f32[32,128]{1,0:T(8,128)S(1)}, f32[32,128]{1,0:T(8,128)}, u32[]{:S(2)}) copy-start(f32[32,128]{1,0:T(8,128)} %param.16) | copy-start | bytes 49156
  46.5 56.0 %collective-permute-start.4 = (bf16[8,128]{1,0:T(8,128)(2,1)S(1)}, bf16[8,128]{1,0:T(8,128)(2,1)S(1)}, u32[]{:S(2)}, u32[]{:S(2)}) collective-permute-start(bf16[8,128]{1,0:T(8,128)(2,1)S(1)} %get-tuple-element.25), channel_id=1, source_target_pairs={{0,8},{4,12},{8,16},{12,20},{16,24},{20,28},{1,9},{5,13},{9,17},{1... | collective-permute-start | bytes 6152 | tf_op jit(solution)/shard_map/ppermute | solution.py:14
  95.4 7.1 %collective-permute-start.5 = (bf16[8,128]{1,0:T(8,128)(2,1)S(1)}, bf16[8,128]{1,0:T(8,128)(2,1)S(1)}, u32[]{:S(2)}, u32[]{:S(2)}) collective-permute-start(bf16[8,128]{1,0:T(8,128)(2,1)S(1)} %get-tuple-element.24), channel_id=1, source_target_pairs={{0,4},{4,8},{8,12},{12,16},{16,20},{20,24},{24,28},{1,5},{5,9},{9,... | collective-permute-start | bytes 6152 | tf_op jit(solution)/shard_map/ppermute | solution.py:14
  99.6 5.5 %collective-permute-start.6 = (bf16[8,128]{1,0:T(8,128)(2,1)S(1)}, bf16[8,128]{1,0:T(8,128)(2,1)S(1)}, u32[]{:S(2)}, u32[]{:S(2)}) collective-permute-start(bf16[8,128]{1,0:T(8,128)(2,1)S(1)} %get-tuple-element.23), channel_id=1, source_target_pairs={{4,0},{8,4},{12,8},{16,12},{20,16},{24,20},{28,24},{5,1},{9,5},{13... | collective-permute-start | bytes 6152 | tf_op jit(solution)/shard_map/ppermute | solution.py:14
  100.9 5.6 %collective-permute-start.7 = (bf16[8,128]{1,0:T(8,128)(2,1)S(1)}, bf16[8,128]{1,0:T(8,128)(2,1)S(1)}, u32[]{:S(2)}, u32[]{:S(2)}) collective-permute-start(bf16[8,128]{1,0:T(8,128)(2,1)S(1)} %get-tuple-element.22), channel_id=1, source_target_pairs={{8,0},{12,4},{16,8},{20,12},{24,16},{28,20},{9,1},{13,5},{17,9},{2... | collective-permute-start | bytes 6152 | tf_op jit(solution)/shard_map/ppermute | solution.py:14
  119.5 37.2 %copy-start.6 = (f32[32,128]{1,0:T(8,128)S(1)}, f32[32,128]{1,0:T(8,128)}, u32[]{:S(2)}) copy-start(f32[32,128]{1,0:T(8,128)} %param.15) | copy-start | bytes 49156
  119.5 63.9 %copy-start.3 = (f32[6,4096]{1,0:T(8,128)S(1)}, f32[6,4096]{1,0:T(8,128)}, u32[]{:S(2)}) copy-start(f32[6,4096]{1,0:T(8,128)} %param.21) | copy-start | bytes 294916
  119.5 64.0 %copy-start.4 = (f32[32,128]{1,0:T(8,128)S(1)}, f32[32,128]{1,0:T(8,128)}, u32[]{:S(2)}) copy-start(f32[32,128]{1,0:T(8,128)} %param.19) | copy-start | bytes 49156
  119.5 64.0 %copy-start.5 = (f32[32,128]{1,0:T(8,128)S(1)}, f32[32,128]{1,0:T(8,128)}, u32[]{:S(2)}) copy-start(f32[32,128]{1,0:T(8,128)} %param.18) | copy-start | bytes 49156
  119.6 105.2 %copy-start.8 = (f32[32,128]{1,0:T(8,128)S(1)}, f32[32,128]{1,0:T(8,128)}, u32[]{:S(2)}) copy-start(f32[32,128]{1,0:T(8,128)} %param.20) | copy-start | bytes 49156
  156.7 68.7 %copy-start.2 = (f32[32,128]{1,0:T(8,128)}, f32[32,128]{1,0:T(8,128)S(1)}, u32[]{:S(2)}) copy-start(f32[32,128]{1,0:T(8,128)S(1)} %get-tuple-element.5) | copy-start | bytes 49156
  157.4 13.0 %collective-permute-start.8 = (f32[8,128]{1,0:T(8,128)S(1)}, f32[8,128]{1,0:T(8,128)S(1)}, u32[]{:S(2)}, u32[]{:S(2)}) collective-permute-start(f32[8,128]{1,0:T(8,128)S(1)} %get-tuple-element.21), channel_id=1, source_target_pairs={{0,8},{4,12},{8,16},{12,20},{16,24},{20,28},{1,9},{5,13},{9,17},{1... | collective-permute-start | bytes 12296 | tf_op jit(solution)/shard_map/ppermute | solution.py:14
  159.5 13.5 %collective-permute-start.9 = (f32[8,128]{1,0:T(8,128)S(1)}, f32[8,128]{1,0:T(8,128)S(1)}, u32[]{:S(2)}, u32[]{:S(2)}) collective-permute-start(f32[8,128]{1,0:T(8,128)S(1)} %get-tuple-element.20), channel_id=1, source_target_pairs={{0,4},{4,8},{8,12},{12,16},{16,20},{20,24},{24,28},{1,5},{5,9},{9,... | collective-permute-start | bytes 12296 | tf_op jit(solution)/shard_map/ppermute | solution.py:14
  161.3 13.1 %collective-permute-start.10 = (f32[8,128]{1,0:T(8,128)S(1)}, f32[8,128]{1,0:T(8,128)S(1)}, u32[]{:S(2)}, u32[]{:S(2)}) collective-permute-start(f32[8,128]{1,0:T(8,128)S(1)} %get-tuple-element.19), channel_id=1, source_target_pairs={{4,0},{8,4},{12,8},{16,12},{20,16},{24,20},{28,24},{5,1},{9,5},{13... | collective-permute-start | bytes 12296 | tf_op jit(solution)/shard_map/ppermute | solution.py:14
  162.6 13.1 %collective-permute-start.11 = (f32[8,128]{1,0:T(8,128)S(1)}, f32[8,128]{1,0:T(8,128)S(1)}, u32[]{:S(2)}, u32[]{:S(2)}) collective-permute-start(f32[8,128]{1,0:T(8,128)S(1)} %get-tuple-element.18), channel_id=1, source_target_pairs={{8,0},{12,4},{16,8},{20,12},{24,16},{28,20},{9,1},{13,5},{17,9},{2... | collective-permute-start | bytes 12296 | tf_op jit(solution)/shard_map/ppermute | solution.py:14
  163.9 11.8 %collective-permute-start.12 = (f32[8,128]{1,0:T(8,128)S(1)}, f32[8,128]{1,0:T(8,128)S(1)}, u32[]{:S(2)}, u32[]{:S(2)}) collective-permute-start(f32[8,128]{1,0:T(8,128)S(1)} %get-tuple-element.17), channel_id=1, source_target_pairs={{0,8},{4,12},{8,16},{12,20},{16,24},{20,28},{1,9},{5,13},{9,17},{1... | collective-permute-start | bytes 12296 | tf_op jit(solution)/shard_map/ppermute | solution.py:14
  170.4 5.3 %collective-permute-start.13 = (f32[8,128]{1,0:T(8,128)S(1)}, f32[8,128]{1,0:T(8,128)S(1)}, u32[]{:S(2)}, u32[]{:S(2)}) collective-permute-start(f32[8,128]{1,0:T(8,128)S(1)} %get-tuple-element.16), channel_id=1, source_target_pairs={{0,4},{4,8},{8,12},{12,16},{16,20},{20,24},{24,28},{1,5},{5,9},{9,... | collective-permute-start | bytes 12296 | tf_op jit(solution)/shard_map/ppermute | solution.py:14
  173.1 6.2 %collective-permute-start.14 = (f32[8,128]{1,0:T(8,128)S(1)}, f32[8,128]{1,0:T(8,128)S(1)}, u32[]{:S(2)}, u32[]{:S(2)}) collective-permute-start(f32[8,128]{1,0:T(8,128)S(1)} %get-tuple-element.15), channel_id=1, source_target_pairs={{4,0},{8,4},{12,8},{16,12},{20,16},{24,20},{28,24},{5,1},{9,5},{13... | collective-permute-start | bytes 12296 | tf_op jit(solution)/shard_map/ppermute | solution.py:14
  174.4 8.3 %collective-permute-start.15 = (f32[8,128]{1,0:T(8,128)S(1)}, f32[8,128]{1,0:T(8,128)S(1)}, u32[]{:S(2)}, u32[]{:S(2)}) collective-permute-start(f32[8,128]{1,0:T(8,128)S(1)} %get-tuple-element.14), channel_id=1, source_target_pairs={{8,0},{12,4},{16,8},{20,12},{24,16},{28,20},{9,1},{13,5},{17,9},{2... | collective-permute-start | bytes 12296 | tf_op jit(solution)/shard_map/ppermute | solution.py:14
Sparse Core Ops, SparseCore 0:
  21.3 20.1 all-gather.2
where the time goes:
time: 233 us; the launch traced here: 232 us
  blocking collectives  106 us (45%)
  starting transfers between devices  42.4 us (18%)
  matrix products  29.2 us (13%)
  local copies, waits for them, and re-layouts  21.3 us (9%)
  between operations  15.3 us (7%)
  waiting for transfers between devices  10.2 us (4%)
  other arithmetic  8.01 us (3%)
    ppermute x16, starting transfers between devices, from_behind(): lax.ppermute(value, axis, [(source, source + steps) for source in range(l...  42.3 us
    psum x1, blocking collectives, local(): summed = lax.psum(partial_value, ('wide', 'narrow'))  40 us
    pmax x1, blocking collectives, local(): rate_top = lax.pmax(jnp.max(cell_rate), ('wide', 'narrow'))  39.9 us
    all_gather x1, blocking collectives, local(): coarse_values = lax.all_gather(owner_values, 'wide', axis=0, tiled=True)  26 us
    dot_general x5, matrix products, block_product(): jnp.einsum('rkij,rkj->ri', matrix, picked, preferred_element_type=jnp.flo...  26 us
    ppermute x16, waiting for transfers between devices, from_behind(): lax.ppermute(value, axis, [(source, source + steps) for source in range(l...  10.2 us
    unnamed x35, local copies, waits for them, and re-layouts  5.47 us
  transfers between devices with their start and end apart: 17, of which 4 were waited for; matrix products, arithmetic and copies ran while one was open for 21% of the time, Pallas kernels for 0%

commit v1 on v0

--- a/solution.py
+++ b/solution.py
@@ -6,6 +6,12 @@
 SWEEPS = 4
 shift_offsets = (2, 1, -1, -2)
 courant = 0.9
+
+
+def trees_use(work_x):
+    prior = jax.lax.psum(work_x, axis_name="narrow")
+    left_arr = jax.lax.psum(prior, axis_name="wide")
+    return left_arr
 
 
 def from_behind(value, axis, steps):
@@ -87,7 +93,7 @@
             / diagonal
         )
     partial_value = jnp.zeros((coarse_total,), jnp.float32).at[coarse_index].add(local_coarse)
-    summed = lax.psum(partial_value, ("wide", "narrow"))
+    summed = trees_use(partial_value)
     owner_block = lax.dynamic_slice_in_dim(
         summed, lax.axis_index("wide") * coarse_width, coarse_width
     )

time: 233 us -> 236 us (1.013)
  blocking collectives: 106 us -> 111 us
  starting transfers between devices: 42.4 us -> 38.9 us
    psum x1 -> x2, blocking collectives: 40 us -> 45.1 us  [the longest x1 34.6 us: trees_use(): left_arr = jax.lax.psum(prior, axis_name='wide')]
    ppermute x16, starting transfers between devices: 42.3 us -> 38.9 us  [from_behind(): lax.ppermute(value, axis, [(source, source + steps) for source in range(l...]
  transfers between devices with their start and end apart: 17 -> 17, of which waited for: 4 -> 4; matrix products, arithmetic and copies ran while one was open for 21% -> 20% of each run, Pallas kernels for 0% -> 0%
where the time goes in v1:
time: 236 us; the launch traced here: 235 us
  blocking collectives  111 us (47%)
  starting transfers between devices  38.9 us (16%)
  matrix products  29.2 us (12%)
  local copies, waits for them, and re-layouts  21.3 us (9%)
  between operations  15.3 us (6%)
  waiting for transfers between devices  11.2 us (5%)
  other arithmetic  8.01 us (3%)
    pmax x1, blocking collectives, local(): rate_top = lax.pmax(jnp.max(cell_rate), ('wide', 'narrow'))  39.9 us
    ppermute x16, starting transfers between devices, from_behind(): lax.ppermute(value, axis, [(source, source + steps) for source in range(l...  38.9 us
    psum x1, blocking collectives, trees_use(): left_arr = jax.lax.psum(prior, axis_name='wide')  34.6 us
    all_gather x1, blocking collectives, local(): coarse_values = lax.all_gather(owner_values, 'wide', axis=0, tiled=True)  26 us
    dot_general x5, matrix products, block_product(): jnp.einsum('rkij,rkj->ri', matrix, picked, preferred_element_type=jnp.flo...  26 us
    ppermute x16, waiting for transfers between devices, from_behind(): lax.ppermute(value, axis, [(source, source + steps) for source in range(l...  11.2 us
    psum x1, blocking collectives, trees_use(): prior = jax.lax.psum(work_x, axis_name='narrow')  10.5 us
    unnamed x35, local copies, waits for them, and re-layouts  5.49 us
  transfers between devices with their start and end apart: 17, of which 4 were waited for; matrix products, arithmetic and copies ran while one was open for 20% of the time, Pallas kernels for 0%

profile of v1, /device:TPU:0, one launch (start us, length us, event | category | flops | bytes accessed | tf_op | source)
XLA Modules:
  0.0 234.9 jit_solution(7274201922021182589)
XLA Ops:
  7.2 0.9 constant_dynamic-update-slice_fusion.4
  8.1 0.7 compare_select_fusion.3
  8.9 0.7 iota_compare_fusion
  10.3 4.9 %collective-permute-start = (bf16[8,128]{1,0:T(8,128)(2,1)S(1)}, bf16[8,128]{1,0:T(8,128)(2,1)S(1)}, u32[]{:S(2)}, u32[]{:S(2)}) collective-permute-start(bf16[8,128]{1,0:T(8,128)(2,1)S(1)} %get-tuple-element.29), channel_id=1, source_target_pairs={{0,8},{4,12},{8,16},{12,20},{16,24},{20,28},{1,9},{5,13},{9,17},{1... | collective-permute-start | bytes 6152 | tf_op jit(solution)/shard_map/ppermute | solution.py:20
  15.2 3.4 %collective-permute-start.1 = (bf16[8,128]{1,0:T(8,128)(2,1)S(1)}, bf16[8,128]{1,0:T(8,128)(2,1)S(1)}, u32[]{:S(2)}, u32[]{:S(2)}) collective-permute-start(bf16[8,128]{1,0:T(8,128)(2,1)S(1)} %get-tuple-element.28), channel_id=1, source_target_pairs={{0,4},{4,8},{8,12},{12,16},{16,20},{20,24},{24,28},{1,5},{5,9},{9,... | collective-permute-start | bytes 6152 | tf_op jit(solution)/shard_map/ppermute | solution.py:20
  18.6 1.3 collective-permute-start.2
  19.9 1.3 collective-permute-start.3
  21.2 0.7 compare_select_fusion.2
  21.9 0.7 compare_select_fusion.1
  22.6 0.7 compare_select_fusion.4
  23.5 3.2 %slice.70 = bf16[64,1,128,128]{3,2,1,0:T(8,128)(2,1)} slice(bf16[64,4,128,128]{3,2,1,0:T(8,128)(2,1)} %param.23), slice={[0:64], [0:1], [0:128], [0:128]} | slice | bytes 4194304 | tf_op jit(solution)/shard_map/slice | solution.py:86
  26.7 5.4 %copy.38 = bf16[64,1,128,128]{0,3,2,1:T(8,128)(2,1)} copy(bf16[64,1,128,128]{3,2,1,0:T(8,128)(2,1)} %slice.70) | data formatting | bytes 4194304
  32.1 2.0 gather_fusion.4
  34.4 0.9 gather_fusion.3
  35.2 5.7 %fusion.8 = f32[64,1,128,1]{2,1,3,0:T(1,128)S(1)} fusion(bf16[64,4,128,128]{3,2,1,0:T(8,128)(2,1)} %param.23, bf16[64,4,128,1]{2,1,0,3:T(4,128)(2,1)S(1)} %bitcast.134), kind=kOutput, calls=%fused_computation.23 | convolution fusion | flops 8388608 | bytes 8486912 | tf_op jit(solution)/shard_map/rkij,rkj->ri/dot_general | solution.py:25
  41.7 0.7 gather_fusion.1
  42.4 3.4 %fusion = f32[32,1,128,1]{2,1,3,0:T(1,128)S(1)} fusion(bf16[64,4,128,128]{3,2,1,0:T(8,128)(2,1)} %param.23, bf16[32,4,128,1]{2,1,0,3:T(4,128)(2,1)S(1)} %bitcast.143), kind=kOutput, calls=%fused_computation.14 | convolution fusion | flops 4194304 | bytes 4243456 | tf_op jit(solution)/shard_map/rkij,rkj->ri/dot_general | solution.py:25
  47.1 2.0 scatter_custom_fusion
  49.1 10.5 %psum.14 = f32[4096]{0:T(1024)S(1)} all-reduce(f32[4096]{0:T(1024)S(1)} %scatter_custom_fusion), channel_id=1, replica_groups=mesh['wide'=8,'narrow'=4] {'narrow'}, use_global_device_ids=true, to_apply=%region_1.2 | all-reduce | flops 4096 | bytes 32768 | tf_op jit(solution)/shard_map/psum | solution.py:12
  59.6 5.9 %collective-permute-start.4 = (bf16[8,128]{1,0:T(8,128)(2,1)S(1)}, bf16[8,128]{1,0:T(8,128)(2,1)S(1)}, u32[]{:S(2)}, u32[]{:S(2)}) collective-permute-start(bf16[8,128]{1,0:T(8,128)(2,1)S(1)} %get-tuple-element.25), channel_id=1, source_target_pairs={{0,8},{4,12},{8,16},{12,20},{16,24},{20,28},{1,9},{5,13},{9,17},{1... | collective-permute-start | bytes 6152 | tf_op jit(solution)/shard_map/ppermute | solution.py:20
  65.6 34.6 %psum.15 = f32[4096]{0:T(1024)S(1)} all-reduce(f32[4096]{0:T(1024)S(1)} %psum.14), channel_id=1, replica_groups=mesh['wide'=8,'narrow'=4] {'wide'}, use_global_device_ids=true, to_apply=%region_2.3 | all-reduce | flops 4096 | bytes 32768 | tf_op jit(solution)/shard_map/psum | solution.py:13
  100.2 1.3 collective-permute-start.5
  101.5 1.3 collective-permute-start.6
  102.8 1.5 collective-permute-start.7
  104.4 2.6 %collective-permute-done.6 = bf16[8,128]{1,0:T(8,128)(2,1)S(1)} collective-permute-done((bf16[8,128]{1,0:T(8,128)(2,1)S(1)}, bf16[8,128]{1,0:T(8,128)(2,1)S(1)}, u32[]{:S(2)}, u32[]{:S(2)}) %collective-permute-start.6) | collective-permute-done | bytes 2080 | tf_op jit(solution)/shard_map/ppermute | solution.py:20
  107.0 2.2 collective-permute-done.7
  109.2 0.9 gather_fusion.5
  110.0 5.6 %fusion.6 = f32[64,1,128,1]{2,1,3,0:T(1,128)S(1)} fusion(bf16[64,4,128,128]{3,2,1,0:T(8,128)(2,1)} %param.23, bf16[64,4,128,1]{2,1,0,3:T(4,128)(2,1)S(1)} %bitcast.135), kind=kOutput, calls=%fused_computation.21 | convolution fusion | flops 8388608 | bytes 8486912 | tf_op jit(solution)/shard_map/rkij,rkj->ri/dot_general | solution.py:25
  115.7 0.9 gather_fusion.6
  116.6 5.6 %fusion.4 = f32[64,1,128,1]{2,1,3,0:T(1,128)S(1)} fusion(bf16[64,4,128,128]{3,2,1,0:T(8,128)(2,1)} %param.23, bf16[64,4,128,1]{2,1,0,3:T(4,128)(2,1)S(1)} %bitcast.136), kind=kOutput, calls=%fused_computation.19 | convolution fusion | flops 8388608 | bytes 8486912 | tf_op jit(solution)/shard_map/rkij,rkj->ri/dot_general | solution.py:25
  122.3 0.9 gather_fusion.7
  123.2 5.6 %fusion.2 = f32[64,1,128,1]{2,1,3,0:T(1,128)S(1)} fusion(bf16[64,4,128,128]{3,2,1,0:T(8,128)(2,1)} %param.23, bf16[64,4,128,1]{2,1,0,3:T(4,128)(2,1)S(1)} %bitcast.133), kind=kOutput, calls=%fused_computation.17 | convolution fusion | flops 8388608 | bytes 8486912 | tf_op jit(solution)/shard_map/rkij,rkj->ri/dot_general | solution.py:25
  128.8 2.2 convolution_bitcast_fusion
  131.0 26.0 %all-gather = bf16[8,1,512]{2,1,0:T(2,128)(2,1)S(1)} all-gather(bf16[1,1,512]{2,1,0:T(2,128)(2,1)S(1)} %convolution_bitcast_fusion), channel_id=1, replica_groups=mesh['wide'=8,'narrow'=4] {'wide'}, dimensions={0}, use_global_device_ids=true | all-gather | bytes 9216 | tf_op jit(solution)/shard_map/all_gather | solution.py:102
  157.1 1.9 gather_fusion.8
  160.1 2.1 collective-permute-start.8
  162.2 1.3 collective-permute-start.9
  163.5 1.3 collective-permute-start.10
  164.8 1.3 collective-permute-start.11
  166.1 6.9 %collective-permute-start.12 = (f32[8,128]{1,0:T(8,128)S(1)}, f32[8,128]{1,0:T(8,128)S(1)}, u32[]{:S(2)}, u32[]{:S(2)}) collective-permute-start(f32[8,128]{1,0:T(8,128)S(1)} %get-tuple-element.17), channel_id=1, source_target_pairs={{0,8},{4,12},{8,16},{12,20},{16,24},{20,28},{1,9},{5,13},{9,17},{1... | collective-permute-start | bytes 12296 | tf_op jit(solution)/shard_map/ppermute | solution.py:20
  173.1 2.5 %collective-permute-start.13 = (f32[8,128]{1,0:T(8,128)S(1)}, f32[8,128]{1,0:T(8,128)S(1)}, u32[]{:S(2)}, u32[]{:S(2)}) collective-permute-start(f32[8,128]{1,0:T(8,128)S(1)} %get-tuple-element.16), channel_id=1, source_target_pairs={{0,4},{4,8},{8,12},{12,16},{16,20},{20,24},{24,28},{1,5},{5,9},{9,... | collective-permute-start | bytes 12296 | tf_op jit(solution)/shard_map/ppermute | solution.py:20
  175.6 1.3 collective-permute-start.14
  176.9 1.3 collective-permute-start.15
  178.3 3.7 %collective-permute-done.14 = f32[8,128]{1,0:T(8,128)S(1)} collective-permute-done((f32[8,128]{1,0:T(8,128)S(1)}, f32[8,128]{1,0:T(8,128)S(1)}, u32[]{:S(2)}, u32[]{:S(2)}) %collective-permute-start.14) | collective-permute-done | bytes 4128 | tf_op jit(solution)/shard_map/ppermute | solution.py:20
  182.0 0.7 gather_fusion.10
  182.7 2.7 %collective-permute-done.15 = f32[8,128]{1,0:T(8,128)S(1)} collective-permute-done((f32[8,128]{1,0:T(8,128)S(1)}, f32[8,128]{1,0:T(8,128)S(1)}, u32[]{:S(2)}, u32[]{:S(2)}) %collective-permute-start.15) | collective-permute-done | bytes 4128 | tf_op jit(solution)/shard_map/ppermute | solution.py:20
  185.4 0.7 gather_fusion.12
  186.9 39.9 %pmax.7 = f32[]{:T(128)} all-reduce(f32[]{:T(128)} %fusion.16), channel_id=1, replica_groups=mesh['wide'=8,'narrow'=4] {'wide','narrow'}, use_global_device_ids=true, to_apply=%region_5.6 | all-reduce | flops 1 | bytes 8 | tf_op jit(solution)/shard_map/pmax | solution.py:125
  (97 shorter events, 6.2 us)
Async XLA Ops:
  7.2 39.3 %copy-start = (bf16[256,4096]{1,0:T(8,128)(2,1)S(1)}, bf16[256,4096]{1,0:T(8,128)(2,1)}, u32[]{:S(2)}) copy-start(bf16[256,4096]{1,0:T(8,128)(2,1)} %param.27) | copy-start | bytes 6291460
  7.2 121.6 %all-gather.3.cloned.1.call-start = ((), (), s32[]{:S(2)}) async-start(), calls=%async_computation | async-start | bytes 1310720 | tf_op jit(solution)/shard_map/all_gather | solution.py:100
  10.3 31.4 %collective-permute-start = (bf16[8,128]{1,0:T(8,128)(2,1)S(1)}, bf16[8,128]{1,0:T(8,128)(2,1)S(1)}, u32[]{:S(2)}, u32[]{:S(2)}) collective-permute-start(bf16[8,128]{1,0:T(8,128)(2,1)S(1)} %get-tuple-element.29), channel_id=1, source_target_pairs={{0,8},{4,12},{8,16},{12,20},{16,24},{20,28},{1,9},{5,13},{9,17},{1... | collective-permute-start | bytes 6152 | tf_op jit(solution)/shard_map/ppermute | solution.py:20
  15.2 26.4 %collective-permute-start.1 = (bf16[8,128]{1,0:T(8,128)(2,1)S(1)}, bf16[8,128]{1,0:T(8,128)(2,1)S(1)}, u32[]{:S(2)}, u32[]{:S(2)}) collective-permute-start(bf16[8,128]{1,0:T(8,128)(2,1)S(1)} %get-tuple-element.28), channel_id=1, source_target_pairs={{0,4},{4,8},{8,12},{12,16},{16,20},{20,24},{24,28},{1,5},{5,9},{9,... | collective-permute-start | bytes 6152 | tf_op jit(solution)/shard_map/ppermute | solution.py:20
  18.6 23.1 %collective-permute-start.2 = (bf16[8,128]{1,0:T(8,128)(2,1)S(1)}, bf16[8,128]{1,0:T(8,128)(2,1)S(1)}, u32[]{:S(2)}, u32[]{:S(2)}) collective-permute-start(bf16[8,128]{1,0:T(8,128)(2,1)S(1)} %get-tuple-element.27), channel_id=1, source_target_pairs={{4,0},{8,4},{12,8},{16,12},{20,16},{24,20},{28,24},{5,1},{9,5},{13... | collective-permute-start | bytes 6152 | tf_op jit(solution)/shard_map/ppermute | solution.py:20
  19.9 21.8 %collective-permute-start.3 = (bf16[8,128]{1,0:T(8,128)(2,1)S(1)}, bf16[8,128]{1,0:T(8,128)(2,1)S(1)}, u32[]{:S(2)}, u32[]{:S(2)}) collective-permute-start(bf16[8,128]{1,0:T(8,128)(2,1)S(1)} %get-tuple-element.26), channel_id=1, source_target_pairs={{8,0},{12,4},{16,8},{20,12},{24,16},{28,20},{9,1},{13,5},{17,9},{2... | collective-permute-start | bytes 6152 | tf_op jit(solution)/shard_map/ppermute | solution.py:20
  26.7 14.2 %copy-start.9 = (s32[6,32]{1,0:T(8,128)S(1)}, s32[6,32]{1,0:T(8,128)}, u32[]{:S(2)}) copy-start(s32[6,32]{1,0:T(8,128)} %param.22) | copy-start | bytes 2308
  26.7 14.3 %copy-start.1 = (f32[32,128]{1,0:T(8,128)S(1)}, f32[32,128]{1,0:T(8,128)}, u32[]{:S(2)}) copy-start(f32[32,128]{1,0:T(8,128)} %param.17) | copy-start | bytes 49156
  32.1 13.7 %copy-start.7 = (f32[32,128]{1,0:T(8,128)S(1)}, f32[32,128]{1,0:T(8,128)}, u32[]{:S(2)}) copy-start(f32[32,128]{1,0:T(8,128)} %param.16) | copy-start | bytes 49156
  59.6 44.7 %collective-permute-start.4 = (bf16[8,128]{1,0:T(8,128)(2,1)S(1)}, bf16[8,128]{1,0:T(8,128)(2,1)S(1)}, u32[]{:S(2)}, u32[]{:S(2)}) collective-permute-start(bf16[8,128]{1,0:T(8,128)(2,1)S(1)} %get-tuple-element.25), channel_id=1, source_target_pairs={{0,8},{4,12},{8,16},{12,20},{16,24},{20,28},{1,9},{5,13},{9,17},{1... | collective-permute-start | bytes 6152 | tf_op jit(solution)/shard_map/ppermute | solution.py:20
  100.2 4.2 %collective-permute-start.5 = (bf16[8,128]{1,0:T(8,128)(2,1)S(1)}, bf16[8,128]{1,0:T(8,128)(2,1)S(1)}, u32[]{:S(2)}, u32[]{:S(2)}) collective-permute-start(bf16[8,128]{1,0:T(8,128)(2,1)S(1)} %get-tuple-element.24), channel_id=1, source_target_pairs={{0,4},{4,8},{8,12},{12,16},{16,20},{20,24},{24,28},{1,5},{5,9},{9,... | collective-permute-start | bytes 6152 | tf_op jit(solution)/shard_map/ppermute | solution.py:20
  101.5 5.5 %collective-permute-start.6 = (bf16[8,128]{1,0:T(8,128)(2,1)S(1)}, bf16[8,128]{1,0:T(8,128)(2,1)S(1)}, u32[]{:S(2)}, u32[]{:S(2)}) collective-permute-start(bf16[8,128]{1,0:T(8,128)(2,1)S(1)} %get-tuple-element.23), channel_id=1, source_target_pairs={{4,0},{8,4},{12,8},{16,12},{20,16},{24,20},{28,24},{5,1},{9,5},{13... | collective-permute-start | bytes 6152 | tf_op jit(solution)/shard_map/ppermute | solution.py:20
  102.8 6.4 %collective-permute-start.7 = (bf16[8,128]{1,0:T(8,128)(2,1)S(1)}, bf16[8,128]{1,0:T(8,128)(2,1)S(1)}, u32[]{:S(2)}, u32[]{:S(2)}) collective-permute-start(bf16[8,128]{1,0:T(8,128)(2,1)S(1)} %get-tuple-element.22), channel_id=1, source_target_pairs={{8,0},{12,4},{16,8},{20,12},{24,16},{28,20},{9,1},{13,5},{17,9},{2... | collective-permute-start | bytes 6152 | tf_op jit(solution)/shard_map/ppermute | solution.py:20
  122.2 37.2 %copy-start.6 = (f32[32,128]{1,0:T(8,128)S(1)}, f32[32,128]{1,0:T(8,128)}, u32[]{:S(2)}) copy-start(f32[32,128]{1,0:T(8,128)} %param.15) | copy-start | bytes 49156
  122.2 63.9 %copy-start.3 = (f32[6,4096]{1,0:T(8,128)S(1)}, f32[6,4096]{1,0:T(8,128)}, u32[]{:S(2)}) copy-start(f32[6,4096]{1,0:T(8,128)} %param.21) | copy-start | bytes 294916
  122.2 64.0 %copy-start.4 = (f32[32,128]{1,0:T(8,128)S(1)}, f32[32,128]{1,0:T(8,128)}, u32[]{:S(2)}) copy-start(f32[32,128]{1,0:T(8,128)} %param.19) | copy-start | bytes 49156
  122.2 64.0 %copy-start.5 = (f32[32,128]{1,0:T(8,128)S(1)}, f32[32,128]{1,0:T(8,128)}, u32[]{:S(2)}) copy-start(f32[32,128]{1,0:T(8,128)} %param.18) | copy-start | bytes 49156
  122.3 105.2 %copy-start.8 = (f32[32,128]{1,0:T(8,128)S(1)}, f32[32,128]{1,0:T(8,128)}, u32[]{:S(2)}) copy-start(f32[32,128]{1,0:T(8,128)} %param.20) | copy-start | bytes 49156
  159.4 68.7 %copy-start.2 = (f32[32,128]{1,0:T(8,128)}, f32[32,128]{1,0:T(8,128)S(1)}, u32[]{:S(2)}) copy-start(f32[32,128]{1,0:T(8,128)S(1)} %get-tuple-element.5) | copy-start | bytes 49156
  160.1 13.0 %collective-permute-start.8 = (f32[8,128]{1,0:T(8,128)S(1)}, f32[8,128]{1,0:T(8,128)S(1)}, u32[]{:S(2)}, u32[]{:S(2)}) collective-permute-start(f32[8,128]{1,0:T(8,128)S(1)} %get-tuple-element.21), channel_id=1, source_target_pairs={{0,8},{4,12},{8,16},{12,20},{16,24},{20,28},{1,9},{5,13},{9,17},{1... | collective-permute-start | bytes 12296 | tf_op jit(solution)/shard_map/ppermute | solution.py:20
  162.2 13.4 %collective-permute-start.9 = (f32[8,128]{1,0:T(8,128)S(1)}, f32[8,128]{1,0:T(8,128)S(1)}, u32[]{:S(2)}, u32[]{:S(2)}) collective-permute-start(f32[8,128]{1,0:T(8,128)S(1)} %get-tuple-element.20), channel_id=1, source_target_pairs={{0,4},{4,8},{8,12},{12,16},{16,20},{20,24},{24,28},{1,5},{5,9},{9,... | collective-permute-start | bytes 12296 | tf_op jit(solution)/shard_map/ppermute | solution.py:20
  163.5 13.4 %collective-permute-start.10 = (f32[8,128]{1,0:T(8,128)S(1)}, f32[8,128]{1,0:T(8,128)S(1)}, u32[]{:S(2)}, u32[]{:S(2)}) collective-permute-start(f32[8,128]{1,0:T(8,128)S(1)} %get-tuple-element.19), channel_id=1, source_target_pairs={{4,0},{8,4},{12,8},{16,12},{20,16},{24,20},{28,24},{5,1},{9,5},{13... | collective-permute-start | bytes 12296 | tf_op jit(solution)/shard_map/ppermute | solution.py:20
  164.8 13.4 %collective-permute-start.11 = (f32[8,128]{1,0:T(8,128)S(1)}, f32[8,128]{1,0:T(8,128)S(1)}, u32[]{:S(2)}, u32[]{:S(2)}) collective-permute-start(f32[8,128]{1,0:T(8,128)S(1)} %get-tuple-element.18), channel_id=1, source_target_pairs={{8,0},{12,4},{16,8},{20,12},{24,16},{28,20},{9,1},{13,5},{17,9},{2... | collective-permute-start | bytes 12296 | tf_op jit(solution)/shard_map/ppermute | solution.py:20
  166.1 12.1 %collective-permute-start.12 = (f32[8,128]{1,0:T(8,128)S(1)}, f32[8,128]{1,0:T(8,128)S(1)}, u32[]{:S(2)}, u32[]{:S(2)}) collective-permute-start(f32[8,128]{1,0:T(8,128)S(1)} %get-tuple-element.17), channel_id=1, source_target_pairs={{0,8},{4,12},{8,16},{12,20},{16,24},{20,28},{1,9},{5,13},{9,17},{1... | collective-permute-start | bytes 12296 | tf_op jit(solution)/shard_map/ppermute | solution.py:20
  173.1 5.2 %collective-permute-start.13 = (f32[8,128]{1,0:T(8,128)S(1)}, f32[8,128]{1,0:T(8,128)S(1)}, u32[]{:S(2)}, u32[]{:S(2)}) collective-permute-start(f32[8,128]{1,0:T(8,128)S(1)} %get-tuple-element.16), channel_id=1, source_target_pairs={{0,4},{4,8},{8,12},{12,16},{16,20},{20,24},{24,28},{1,5},{5,9},{9,... | collective-permute-start | bytes 12296 | tf_op jit(solution)/shard_map/ppermute | solution.py:20
  175.6 6.4 %collective-permute-start.14 = (f32[8,128]{1,0:T(8,128)S(1)}, f32[8,128]{1,0:T(8,128)S(1)}, u32[]{:S(2)}, u32[]{:S(2)}) collective-permute-start(f32[8,128]{1,0:T(8,128)S(1)} %get-tuple-element.15), channel_id=1, source_target_pairs={{4,0},{8,4},{12,8},{16,12},{20,16},{24,20},{28,24},{5,1},{9,5},{13... | collective-permute-start | bytes 12296 | tf_op jit(solution)/shard_map/ppermute | solution.py:20
  176.9 8.5 %collective-permute-start.15 = (f32[8,128]{1,0:T(8,128)S(1)}, f32[8,128]{1,0:T(8,128)S(1)}, u32[]{:S(2)}, u32[]{:S(2)}) collective-permute-start(f32[8,128]{1,0:T(8,128)S(1)} %get-tuple-element.14), channel_id=1, source_target_pairs={{8,0},{12,4},{16,8},{20,12},{24,16},{28,20},{9,1},{13,5},{17,9},{2... | collective-permute-start | bytes 12296 | tf_op jit(solution)/shard_map/ppermute | solution.py:20
Sparse Core Ops, SparseCore 0:
  21.3 20.1 all-gather.2
